TPU v7x, 256 devices: a whole 4x4x8 slice. The times are simulated.
256 devices in a mesh: ctx: 8 (over x, y_lo), mp: 32 (over z, y_hi, core).
Axes of the slice: x: 4, y: 4 (y_hi: 2, y_lo: 2; y = y_hi * 2 + y_lo), z: 8, core: 2. Of those that a mesh axis runs over, the one named last changes fastest.
Arguments:
- residual_in: bfloat16 [4096, 8192], P('ctx', 'mp'), may hold values from -4 to 4
- query_rows: bfloat16 [4096, 8192], P('ctx', 'mp'), may hold values from -5 to 5
- key_rows: bfloat16 [4096, 8192], P('ctx', 'mp'), may hold values from -5 to 5
- value_rows: bfloat16 [4096, 8192], P('ctx', 'mp'), may hold values from -5 to 5
- out_weight: bfloat16 [8192, 8192], P('mp'), may hold values from -1 to 1
- gate_in: bfloat16 [4096, 8192], P('ctx', 'mp'), may hold values from -5 to 5
- gate_out: bfloat16 [4096, 8192], P('ctx', 'mp'), may hold values from -5 to 5
- short_taps: float32 [3, 8192], P(None, 'mp'), may hold values from -3 to 3
- decay_rates: float32 [16, 8192], P(None, 'mp'), may hold values from 4.8828126e-05 to 0.03
- residues: float32 [16, 8192], P(None, 'mp'), may hold values from -0.15 to 0.15
- skip_gain: float32 [8192], P('mp'), may hold values from -4 to 4
Outputs:
- attended: bfloat16 [4096, 8192], P('ctx', 'mp')
- hyena_out: bfloat16 [4096, 8192], P('ctx', 'mp')
All inputs are finite; a program needn't handle non-finite values.
Results may differ from a plain program's by a relative error of at most 0.02.
Values may be sent and summed in bfloat16 or wider, within the bound.
No kernel may reach another device: no remote copies, remote signals or barrier semaphores. Data moves between devices by JAX's collectives and lax.ppermute only.
A program may use at most 128 MiB of HBM per device.

v0:
```python
import jax
import jax.numpy as jnp
from jax import lax
from jax.sharding import PartitionSpec as P

HD = 128
BLOCK = 64
masked_floor = -1e30


def from_behind(value, axis, steps):
    count = lax.axis_size(axis)
    leading, last = (max(0, -steps), min(count, count - steps))
    return lax.ppermute(value, axis, [(source, source + steps) for source in range(leading, last)])


def modal_tables(decay_rates, residues, block):
    width = decay_rates.shape[1]
    lags = jnp.arange(block).astype(jnp.float32)
    lag_diff = lags[:, None] - lags[None, :]
    causal = lag_diff >= 0
    safe_diff = jnp.maximum(lag_diff, 0.0)

    def add_pole(total, pole):
        rate, residue = pole
        return (
            total + residue[None, None, :] * jnp.exp(-rate[None, None, :] * safe_diff[:, :, None]),
            None,
        )

    toeplitz, _ = lax.scan(
        add_pole, jnp.zeros((block, block, width), jnp.float32), (decay_rates, residues)
    )
    toeplitz = jnp.where(causal[:, :, None], toeplitz, 0.0)
    powers = jnp.exp(-decay_rates[None] * lags[:, None, None])
    inward = jnp.exp(-decay_rates[None] * (block - lags)[:, None, None])
    return (toeplitz, powers, inward)


def modal_conv(signal, decay_rates, residues, block):
    length, width = signal.shape
    toeplitz, powers, inward = modal_tables(decay_rates, residues, block)
    highest = lax.Precision.HIGHEST
    span = jnp.exp(-decay_rates * block)

    def modal_step(state, piece):
        local = jnp.einsum("ijc,jc->ic", toeplitz, piece, precision=highest)
        carried = jnp.einsum("inc,nc->ic", powers, residues * state, precision=highest)
        state = span * state + jnp.einsum("jnc,jc->nc", inward, piece, precision=highest)
        return (state, local + carried)

    start_state = jnp.zeros((decay_rates.shape[0], width), jnp.float32)
    state, result = lax.scan(modal_step, start_state, signal.reshape(length // block, block, width))
    return (result.reshape(length, width), state)


def attend(groups, key_rows, value_rows):
    width = key_rows.shape[1]
    heads = width // HD
    scale = HD ** (-0.5)
    query_sets = [(rows_q.reshape(rows_q.shape[0], heads, HD), pos_q) for rows_q, pos_q in groups]

    def update(state, queries, query_pos, keys_here, values_here, key_pos):
        running_top, running_total, running_sum = state
        scores = (
            jnp.einsum("qhd,khd->hqk", queries, keys_here, preferred_element_type=jnp.float32)
            * scale
        )
        allowed = (key_pos[None, :] <= query_pos[:, None])[None]
        masked = jnp.where(allowed, scores, masked_floor)
        new_top = jnp.maximum(running_top, jnp.max(masked, axis=-1))
        weights = jnp.where(allowed, jnp.exp(masked - new_top[..., None]), 0.0)
        rescale = jnp.exp(running_top - new_top)
        new_total = running_total * rescale + jnp.sum(weights, axis=-1)
        new_sum = running_sum * rescale[..., None] + jnp.einsum(
            "hqk,khd->hqd",
            weights.astype(jnp.bfloat16),
            values_here,
            preferred_element_type=jnp.float32,
        )
        return (new_top, new_total, new_sum)

    initial = tuple(
        (
            (
                jnp.full((heads, pos_q.shape[0]), masked_floor, jnp.float32),
                jnp.zeros((heads, pos_q.shape[0]), jnp.float32),
                jnp.zeros((heads, pos_q.shape[0], HD), jnp.float32),
            )
            for rows_q, pos_q in groups
        )
    )
    pieces = (
        lax.all_gather(key_rows, "ctx", axis=0, tiled=True),
        lax.all_gather(value_rows, "ctx", axis=0, tiled=True),
    )
    count = pieces[0].shape[0]
    blocks = count // count
    keys_all = pieces[0].reshape(blocks, count, heads, HD)
    values_all = pieces[1].reshape(blocks, count, heads, HD)
    index_rows = jnp.arange(count)
    pos_all = index_rows.reshape(blocks, count)

    def fold_step(states, block):
        keys_here, values_here, key_pos = block
        return (
            tuple(
                (
                    update(
                        states[g],
                        query_sets[g][0],
                        query_sets[g][1],
                        keys_here,
                        values_here,
                        key_pos,
                    )
                    for g in range(len(query_sets))
                )
            ),
            None,
        )

    result, _ = lax.scan(fold_step, initial, (keys_all, values_all, pos_all))
    return [(final[2] / final[1][..., None]).astype(jnp.bfloat16) for final in result]


def per_device(
    residual_in,
    query_rows,
    key_rows,
    value_rows,
    out_weight,
    gate_in,
    gate_out,
    short_taps,
    decay_rates,
    residues,
    skip_gain,
):
    rows = residual_in.shape[0]
    width = residual_in.shape[1]
    segment = lax.axis_index("ctx")
    query_pos = segment * rows + jnp.arange(rows)
    heads_out = attend([(query_rows, query_pos)], key_rows, value_rows)[0]
    heads = heads_out.shape[0]
    columns = out_weight.reshape(heads, HD, width * lax.axis_size("mp"))
    projected = lax.psum_scatter(
        jnp.einsum("hqd,hdc->cq", heads_out, columns, preferred_element_type=jnp.float32).astype(
            jnp.bfloat16
        ),
        "mp",
        scatter_dimension=0,
        tiled=True,
    ).astype(jnp.float32)
    attended = (residual_in.astype(jnp.float32) + projected.T).astype(jnp.bfloat16)
    taps = short_taps.shape[0]
    rim = from_behind(attended[rows - (taps - 1) :], "ctx", 1)
    extended = jnp.concatenate([rim, attended], axis=0).astype(jnp.float32)
    shortconv = jnp.zeros((rows, width), jnp.float32)
    for tap in range(taps):
        shortconv = (
            shortconv + short_taps[tap][None, :] * extended[taps - 1 - tap : taps - 1 - tap + rows]
        )
    signal = gate_in.astype(jnp.float32) * shortconv
    local, final_state = modal_conv(signal, decay_rates, residues, BLOCK)
    highest = lax.Precision.HIGHEST
    lag_rows = jnp.arange(rows).astype(jnp.float32)
    long_powers = residues[None] * jnp.exp(-decay_rates[None] * lag_rows[:, None, None])
    later_count = rows * lax.axis_size("ctx") // rows
    later_index = jnp.arange(later_count)
    gap = jnp.maximum((later_index - segment - 1) * rows, 0).astype(jnp.float32)
    factor = jnp.exp(-decay_rates[None] * gap[:, None, None])
    states = jnp.where((later_index > segment)[:, None, None], factor * final_state[None], 0.0)
    carried = lax.psum_scatter(
        jnp.einsum("inc,jnc->jic", long_powers, states, precision=highest)
        .reshape(rows * lax.axis_size("ctx"), width)
        .astype(jnp.bfloat16),
        "ctx",
        scatter_dimension=0,
        tiled=True,
    ).astype(jnp.float32)
    hyena_out = (
        gate_out.astype(jnp.float32) * (local + carried + skip_gain[None, :] * signal)
    ).astype(jnp.bfloat16)
    return (attended, hyena_out)


def solution(mesh):
    in_specs = (
        P("ctx", "mp"),
        P("ctx", "mp"),
        P("ctx", "mp"),
        P("ctx", "mp"),
        P("mp", None),
        P("ctx", "mp"),
        P("ctx", "mp"),
        P(None, "mp"),
        P(None, "mp"),
        P(None, "mp"),
        P("mp"),
    )
    out_specs = (P("ctx", "mp"), P("ctx", "mp"))
    return jax.shard_map(
        per_device, mesh=mesh, in_specs=in_specs, out_specs=out_specs, check_vma=False
    )
```

profile of v0, /device:TPU:26, one launch (start us, length us, event | category | flops | bytes accessed | tf_op | source)
XLA Modules:
  0.0 405.1 jit_solution(8935362246046610650)
XLA Ops:
  7.2 1.8 copy.19
  9.1 0.7 all-gather.5.cloned.1.call-update
  9.9 0.8 fusion.64
  10.8 0.7 fusion.63
  11.6 1.7 iota_compare_fusion
  13.2 54.2 %all-gather.3.cloned.1.call-done = bf16[4096,256]{0,1:T(8,128)(2,1)} async-done(((bf16[512,256]{0,1:T(8,128)(2,1)}), bf16[4096,256]{0,1:T(8,128)(2,1)}) %all-gather.3.cloned.1.call-update) | async-done | bytes 2097168 | tf_op jit(solution)/shard_map/all_gather | solution.py:94
  67.4 5.4 %fusion.6 = (f32[2,512]{1,0:T(2,128)S(1)}, f32[2,512,4096]{2,1,0:T(8,128)S(1)}) fusion(pred[512,4096]{1,0:T(8,128)(4,1)S(1)} %iota_compare_fusion, bf16[4096,2,128]{0,2,1:T(8,128)(2,1)} %bitcast.107, bf16[512,256]{1,0:T(8,128)(2,1)S(1)} %copy-done), kind=kOutput, calls=%fused_computation.17 | convolution fusion | flops 1086323712 | bytes 21237760 | tf_op jit(solution)/shard_map/while/body/eval_jaxpr/qhd,khd->hqk/dot_general | solution.py:66
  72.9 5.3 %fusion.7 = f32[2,512]{1,0:T(2,128)S(1)} fusion(f32[2,512,4096]{2,1,0:T(8,128)S(1)} %get-tuple-element.265, f32[2,512]{1,0:T(2,128)S(1)} %broadcast_maximum_fusion, pred[512,4096]{1,0:T(8,128)(4,1)S(1)} %iota_compare_fusion), kind=kLoop, calls=%fused_computation.18 | loop fusion | flops 20970496 | bytes 18882560 | tf_op jit(solution)/shard_map/while/body/eval_jaxpr/reduce_sum | solution.py:74
  78.6 44.5 %all-gather.5.cloned.1.call-done = bf16[4096,256]{1,0:T(8,128)(2,1)} async-done(((bf16[512,256]{1,0:T(8,128)(2,1)}), bf16[4096,256]{1,0:T(8,128)(2,1)}) %all-gather.5.cloned.1.call-update) | async-done | bytes 2097168 | tf_op jit(solution)/shard_map/all_gather | solution.py:95
  123.1 15.0 %fusion.9 = bf16[8192,512]{0,1:T(8,128)(2,1)} fusion(bf16[2,128,8192]{2,1,0:T(8,128)(2,1)} %bitcast.106, f32[2,512,4096]{2,1,0:T(8,128)} %copy-done.1, f32[2,512]{1,0:T(2,128)S(1)} %broadcast_maximum_fusion, pred[512,4096]{1,0:T(8,128)(4,1)S(1)} %iota_compare_fusion, f32[2,512]{1,0:T(2,128)S(1)} %get-tuple-element.263, ...), kind=kOutput, calls=%fused_computation.20 | convolution fusion | flops 3246784512 | bytes 33566720 | tf_op jit(solution)/shard_map/hqd,hdc->cq/dot_general | solution.py:148
  138.2 0.6 copy-done.3
  138.8 77.4 %while.32 = (s32[]{:T(128)}, f32[64,64,256]{2,1,0:T(8,128)}, f32[16,256]{1,0:T(8,128)S(1)}, f32[16,256]{1,0:T(8,128)}, f32[64]{0:T(128)S(1)}, /*index=5*/s32[]{:T(128)}, s32[]{:T(128)}) while((s32[]{:T(128)}, f32[64,64,256]{2,1,0:T(8,128)}, f32[16,256]{1,0:T(8,128)S(1)}, f32[16,256]{1,0:T(8,128)}, f32[64]{0:T(128)S(1)}, ...), condition=%wide.region_4.5_spmd.clone, body=%wide.region_3.4_spmd.clone.sunk | while | flops 4202755 | bytes 8427867 | solution.py:31
  138.8 0.7 dynamic-slice_negate_fusion.2
  139.6 2.5 select_add_fusion.2
  142.1 0.7 dynamic-slice_negate_fusion.2
  142.9 4.1 %select_add_fusion.2 = f32[64,64,256]{2,1,0:T(8,128)} fusion(f32[64,64,256]{2,1,0:T(8,128)} %get-tuple-element.374, f32[64,64]{1,0:T(8,128)S(1)} %subtract_maximum_fusion.2, f32[256]{0:T(256)S(1)} %bitcast.101, f32[256]{0:T(256)S(1)} %bitcast.102, pred[]{:T(512)S(6)} %compare.8), kind=kLoop, calls=%fused_computation.3.clone.1 | loop fusion | flops 4194304 | bytes 8407041 | tf_op jit(solution)/shard_map/while/body/eval_jaxpr/add | solution.py:27
  146.9 0.7 dynamic-slice_negate_fusion.2
  147.7 4.1 %select_add_fusion.2 = f32[64,64,256]{2,1,0:T(8,128)} fusion(f32[64,64,256]{2,1,0:T(8,128)} %get-tuple-element.374, f32[64,64]{1,0:T(8,128)S(1)} %subtract_maximum_fusion.2, f32[256]{0:T(256)S(1)} %bitcast.101, f32[256]{0:T(256)S(1)} %bitcast.102, pred[]{:T(512)S(6)} %compare.8), kind=kLoop, calls=%fused_computation.3.clone.1 | loop fusion | flops 4194304 | bytes 8407041 | tf_op jit(solution)/shard_map/while/body/eval_jaxpr/add | solution.py:27
  151.8 0.7 dynamic-slice_negate_fusion.2
  152.6 4.3 %select_add_fusion.2 = f32[64,64,256]{2,1,0:T(8,128)} fusion(f32[64,64,256]{2,1,0:T(8,128)} %get-tuple-element.374, f32[64,64]{1,0:T(8,128)S(1)} %subtract_maximum_fusion.2, f32[256]{0:T(256)S(1)} %bitcast.101, f32[256]{0:T(256)S(1)} %bitcast.102, pred[]{:T(512)S(6)} %compare.8), kind=kLoop, calls=%fused_computation.3.clone.1 | loop fusion | flops 4194304 | bytes 8407041 | tf_op jit(solution)/shard_map/while/body/eval_jaxpr/add | solution.py:27
  156.9 0.7 dynamic-slice_negate_fusion.2
  157.7 4.3 %select_add_fusion.2 = f32[64,64,256]{2,1,0:T(8,128)} fusion(f32[64,64,256]{2,1,0:T(8,128)} %get-tuple-element.374, f32[64,64]{1,0:T(8,128)S(1)} %subtract_maximum_fusion.2, f32[256]{0:T(256)S(1)} %bitcast.101, f32[256]{0:T(256)S(1)} %bitcast.102, pred[]{:T(512)S(6)} %compare.8), kind=kLoop, calls=%fused_computation.3.clone.1 | loop fusion | flops 4194304 | bytes 8407041 | tf_op jit(solution)/shard_map/while/body/eval_jaxpr/add | solution.py:27
  161.9 0.7 dynamic-slice_negate_fusion.2
  162.7 4.3 %select_add_fusion.2 = f32[64,64,256]{2,1,0:T(8,128)} fusion(f32[64,64,256]{2,1,0:T(8,128)} %get-tuple-element.374, f32[64,64]{1,0:T(8,128)S(1)} %subtract_maximum_fusion.2, f32[256]{0:T(256)S(1)} %bitcast.101, f32[256]{0:T(256)S(1)} %bitcast.102, pred[]{:T(512)S(6)} %compare.8), kind=kLoop, calls=%fused_computation.3.clone.1 | loop fusion | flops 4194304 | bytes 8407041 | tf_op jit(solution)/shard_map/while/body/eval_jaxpr/add | solution.py:27
  167.0 0.7 dynamic-slice_negate_fusion.2
  167.8 4.3 %select_add_fusion.2 = f32[64,64,256]{2,1,0:T(8,128)} fusion(f32[64,64,256]{2,1,0:T(8,128)} %get-tuple-element.374, f32[64,64]{1,0:T(8,128)S(1)} %subtract_maximum_fusion.2, f32[256]{0:T(256)S(1)} %bitcast.101, f32[256]{0:T(256)S(1)} %bitcast.102, pred[]{:T(512)S(6)} %compare.8), kind=kLoop, calls=%fused_computation.3.clone.1 | loop fusion | flops 4194304 | bytes 8407041 | tf_op jit(solution)/shard_map/while/body/eval_jaxpr/add | solution.py:27
  172.0 0.7 dynamic-slice_negate_fusion.2
  172.8 4.3 %select_add_fusion.2 = f32[64,64,256]{2,1,0:T(8,128)} fusion(f32[64,64,256]{2,1,0:T(8,128)} %get-tuple-element.374, f32[64,64]{1,0:T(8,128)S(1)} %subtract_maximum_fusion.2, f32[256]{0:T(256)S(1)} %bitcast.101, f32[256]{0:T(256)S(1)} %bitcast.102, pred[]{:T(512)S(6)} %compare.8), kind=kLoop, calls=%fused_computation.3.clone.1 | loop fusion | flops 4194304 | bytes 8407041 | tf_op jit(solution)/shard_map/while/body/eval_jaxpr/add | solution.py:27
  177.1 0.7 dynamic-slice_negate_fusion.2
  177.9 4.3 %select_add_fusion.2 = f32[64,64,256]{2,1,0:T(8,128)} fusion(f32[64,64,256]{2,1,0:T(8,128)} %get-tuple-element.374, f32[64,64]{1,0:T(8,128)S(1)} %subtract_maximum_fusion.2, f32[256]{0:T(256)S(1)} %bitcast.101, f32[256]{0:T(256)S(1)} %bitcast.102, pred[]{:T(512)S(6)} %compare.8), kind=kLoop, calls=%fused_computation.3.clone.1 | loop fusion | flops 4194304 | bytes 8407041 | tf_op jit(solution)/shard_map/while/body/eval_jaxpr/add | solution.py:27
  182.1 0.7 dynamic-slice_negate_fusion.2
  182.9 4.1 %select_add_fusion.2 = f32[64,64,256]{2,1,0:T(8,128)} fusion(f32[64,64,256]{2,1,0:T(8,128)} %get-tuple-element.374, f32[64,64]{1,0:T(8,128)S(1)} %subtract_maximum_fusion.2, f32[256]{0:T(256)S(1)} %bitcast.101, f32[256]{0:T(256)S(1)} %bitcast.102, pred[]{:T(512)S(6)} %compare.8), kind=kLoop, calls=%fused_computation.3.clone.1 | loop fusion | flops 4194304 | bytes 8407041 | tf_op jit(solution)/shard_map/while/body/eval_jaxpr/add | solution.py:27
  187.0 0.7 dynamic-slice_negate_fusion.2
  187.7 4.1 %select_add_fusion.2 = f32[64,64,256]{2,1,0:T(8,128)} fusion(f32[64,64,256]{2,1,0:T(8,128)} %get-tuple-element.374, f32[64,64]{1,0:T(8,128)S(1)} %subtract_maximum_fusion.2, f32[256]{0:T(256)S(1)} %bitcast.101, f32[256]{0:T(256)S(1)} %bitcast.102, pred[]{:T(512)S(6)} %compare.8), kind=kLoop, calls=%fused_computation.3.clone.1 | loop fusion | flops 4194304 | bytes 8407041 | tf_op jit(solution)/shard_map/while/body/eval_jaxpr/add | solution.py:27
  191.8 0.7 dynamic-slice_negate_fusion.2
  192.6 4.2 %select_add_fusion.2 = f32[64,64,256]{2,1,0:T(8,128)} fusion(f32[64,64,256]{2,1,0:T(8,128)} %get-tuple-element.374, f32[64,64]{1,0:T(8,128)S(1)} %subtract_maximum_fusion.2, f32[256]{0:T(256)S(1)} %bitcast.101, f32[256]{0:T(256)S(1)} %bitcast.102, pred[]{:T(512)S(6)} %compare.8), kind=kLoop, calls=%fused_computation.3.clone.1 | loop fusion | flops 4194304 | bytes 8407041 | tf_op jit(solution)/shard_map/while/body/eval_jaxpr/add | solution.py:27
  196.8 0.7 dynamic-slice_negate_fusion.2
  197.6 4.1 %select_add_fusion.2 = f32[64,64,256]{2,1,0:T(8,128)} fusion(f32[64,64,256]{2,1,0:T(8,128)} %get-tuple-element.374, f32[64,64]{1,0:T(8,128)S(1)} %subtract_maximum_fusion.2, f32[256]{0:T(256)S(1)} %bitcast.101, f32[256]{0:T(256)S(1)} %bitcast.102, pred[]{:T(512)S(6)} %compare.8), kind=kLoop, calls=%fused_computation.3.clone.1 | loop fusion | flops 4194304 | bytes 8407041 | tf_op jit(solution)/shard_map/while/body/eval_jaxpr/add | solution.py:27
  201.6 0.7 dynamic-slice_negate_fusion.2
  202.4 4.1 %select_add_fusion.2 = f32[64,64,256]{2,1,0:T(8,128)} fusion(f32[64,64,256]{2,1,0:T(8,128)} %get-tuple-element.374, f32[64,64]{1,0:T(8,128)S(1)} %subtract_maximum_fusion.2, f32[256]{0:T(256)S(1)} %bitcast.101, f32[256]{0:T(256)S(1)} %bitcast.102, pred[]{:T(512)S(6)} %compare.8), kind=kLoop, calls=%fused_computation.3.clone.1 | loop fusion | flops 4194304 | bytes 8407041 | tf_op jit(solution)/shard_map/while/body/eval_jaxpr/add | solution.py:27
  206.5 0.7 dynamic-slice_negate_fusion.2
  207.3 4.1 %select_add_fusion.2 = f32[64,64,256]{2,1,0:T(8,128)} fusion(f32[64,64,256]{2,1,0:T(8,128)} %get-tuple-element.374, f32[64,64]{1,0:T(8,128)S(1)} %subtract_maximum_fusion.2, f32[256]{0:T(256)S(1)} %bitcast.101, f32[256]{0:T(256)S(1)} %bitcast.102, pred[]{:T(512)S(6)} %compare.8), kind=kLoop, calls=%fused_computation.3.clone.1 | loop fusion | flops 4194304 | bytes 8407041 | tf_op jit(solution)/shard_map/while/body/eval_jaxpr/add | solution.py:27
  211.3 0.7 dynamic-slice_negate_fusion.2
  212.1 4.1 %select_add_fusion.2 = f32[64,64,256]{2,1,0:T(8,128)} fusion(f32[64,64,256]{2,1,0:T(8,128)} %get-tuple-element.374, f32[64,64]{1,0:T(8,128)S(1)} %subtract_maximum_fusion.2, f32[256]{0:T(256)S(1)} %bitcast.101, f32[256]{0:T(256)S(1)} %bitcast.102, pred[]{:T(512)S(6)} %compare.8), kind=kLoop, calls=%fused_computation.3.clone.1 | loop fusion | flops 4194304 | bytes 8407041 | tf_op jit(solution)/shard_map/while/body/eval_jaxpr/add | solution.py:27
  216.2 4.0 broadcast_select_fusion
  220.2 72.1 %reduce-scatter.3.cloned.1.call-done = bf16[256,512]{0,1:T(8,128)(2,1)} async-done(((bf16[8192,512]{0,1:T(8,128)(2,1)}), bf16[256,512]{0,1:T(8,128)(2,1)}) %reduce-scatter.3.cloned.1.call-update) | async-done | bytes 262160 | tf_op jit(solution)/shard_map/reduce_scatter | solution.py:147
  292.3 1.0 fusion.49
  293.4 3.5 collective-permute-start
  296.9 0.8 copy.24
  297.7 0.8 copy.22
  299.1 32.8 %while.33 = (s32[]{:T(128)}, f32[16,256]{1,0:T(8,128)S(1)}, f32[8,64,256]{2,1,0:T(8,128)}, f32[16,256]{1,0:T(8,128)S(1)}, f32[8,64,256]{2,1,0:T(8,128)S(1)}, /*i...) while((s32[]{:T(128)}, f32[16,256]{1,0:T(8,128)S(1)}, ...), condition=%wide.region_6.7_spmd.clone.clone.clone, body=%wide.region_5.6_spmd.clone.clone.clone.sunk | while | flops 3665923 | bytes 4949123 | solution.py:53
  299.8 2.8 multiply_reduce_fusion.7
  303.9 2.8 multiply_reduce_fusion.7
  308.0 2.8 multiply_reduce_fusion.7
  312.1 2.8 multiply_reduce_fusion.7
  316.2 2.8 multiply_reduce_fusion.7
  320.3 2.8 multiply_reduce_fusion.7
  324.4 2.8 multiply_reduce_fusion.7
  327.2 0.6 bitcast_dynamic-update-slice_fusion.2
  328.5 2.8 multiply_reduce_fusion.7
  332.0 6.8 %convert_bitcast_fusion = bf16[8,512,256]{1,0,2:T(8,128)(2,1)S(1)} fusion(f32[512]{0:T(512)S(1)} %iota_convert_fusion, f32[16,256]{0,1:T(8,128)} %copy.22, f32[16,256]{0,1:T(8,128)S(1)} %copy-done.7, f32[16,256]{0,1:T(8,128)S(1)} %copy.23, f32[8]{0:T(128)S(1)} %maximum_convert_fusion.1, pred[8]{0:T(512)(128)(4,1)S(1)} %iota_compare_fusion.1), kind=kOutput, calls=%fused_computation.33 | convolution fusion | flops 206667776 | bytes 2148392 | tf_op jit(solution)/shard_map/inc,jnc->jic/dot_general | solution.py:175
  338.9 2.8 copy.26
  341.7 55.0 %reduce-scatter.5.cloned.1.call-done = bf16[512,256]{1,0:T(8,128)(2,1)} async-done(((bf16[4096,256]{1,0:T(8,128)(2,1)}), bf16[512,256]{1,0:T(8,128)(2,1)}) %reduce-scatter.5.cloned.1.call-update) | async-done | bytes 262160 | tf_op jit(solution)/shard_map/reduce_scatter | solution.py:174
  396.6 1.9 fusion.48
  (96 shorter events, 12.0 us)
Async XLA Ops:
  7.2 60.3 %copy-start = (bf16[512,256]{1,0:T(8,128)(2,1)S(1)}, bf16[512,256]{1,0:T(8,128)(2,1)}, u32[]{:S(2)}) copy-start(bf16[512,256]{1,0:T(8,128)(2,1)} %param.16) | copy-start | bytes 786436
  7.2 60.3 %all-gather.3.cloned.1.call-start = ((), (), s32[]{:S(2)}) async-start(), calls=%async_computation.2 | async-start | bytes 2359296 | tf_op jit(solution)/shard_map/all_gather | solution.py:94
  9.1 114.1 %all-gather.5.cloned.1.call-start = ((), (), s32[]{:S(2)}) async-start(), calls=%async_computation.3 | async-start | bytes 2359296 | tf_op jit(solution)/shard_map/all_gather | solution.py:95
  9.8 282.5 %reduce-scatter.3.cloned.1.call-start = ((), (), s32[]{:S(2)}) async-start(), calls=%async_computation.4 | async-start | bytes 8650752 | tf_op jit(solution)/shard_map/reduce_scatter | solution.py:147
  72.9 5.7 %copy-start.1 = (f32[2,512,4096]{2,1,0:T(8,128)}, f32[2,512,4096]{2,1,0:T(8,128)S(1)}, u32[]{:S(2)}) copy-start(f32[2,512,4096]{2,1,0:T(8,128)S(1)} %get-tuple-element.265) | copy-start | bytes 50331652
  138.1 0.7 copy-start.3
  138.1 258.5 %reduce-scatter.5.cloned.1.call-start = ((), (), s32[]{:S(2)}) async-start(), calls=%async_computation.5 | async-start | bytes 2359296 | tf_op jit(solution)/shard_map/reduce_scatter | solution.py:174
  216.2 76.1 %copy-start.5 = (bf16[512,256]{1,0:T(8,128)(2,1)S(1)}, bf16[512,256]{1,0:T(8,128)(2,1)}, u32[]{:S(2)}) copy-start(bf16[512,256]{1,0:T(8,128)(2,1)} %param.15) | copy-start | bytes 786436
  216.2 82.7 %copy-start.6 = (bf16[512,256]{1,0:T(8,128)(2,1)S(1)}, bf16[512,256]{1,0:T(8,128)(2,1)}, u32[]{:S(2)}) copy-start(bf16[512,256]{1,0:T(8,128)(2,1)} %param.20) | copy-start | bytes 786436
  293.4 5.8 %copy-start.2 = (bf16[512,256]{1,0:T(8,128)(2,1)}, bf16[512,256]{1,0:T(8,128)(2,1)S(1)}, u32[]{:S(2)}) copy-start(bf16[512,256]{1,0:T(8,128)(2,1)S(1)} %fusion.49) | copy-start | bytes 786436
  293.4 5.5 %collective-permute-start = (bf16[2,256]{1,0:T(2,128)(2,1)S(1)}, bf16[2,256]{1,0:T(2,128)(2,1)S(1)}, u32[]{:S(2)}, u32[]{:S(2)}) collective-permute-start(bf16[2,256]{1,0:T(2,128)(2,1)S(1)} %slice.28), channel_id=1, source_target_pairs={{0,32},{32,64},{64,96},{96,128},{128,160},{160,192},{192,224},{1,3... | collective-permute-start | bytes 3080 | tf_op jit(solution)/shard_map/ppermute | solution.py:14
  299.1 32.9 %copy-start.7 = (f32[16,256]{0,1:T(8,128)S(1)}, f32[16,256]{0,1:T(8,128)}, u32[]{:S(2)}) copy-start(f32[16,256]{0,1:T(8,128)} %copy.24) | copy-start | bytes 49156
  338.9 57.8 %copy-start.4 = (f32[8,64,256]{2,1,0:T(8,128)S(1)}, f32[8,64,256]{2,1,0:T(8,128)}, u32[]{:S(2)}) copy-start(f32[8,64,256]{2,1,0:T(8,128)} %get-tuple-element.105) | copy-start | bytes 1572868
  338.9 57.8 %copy-start.8 = (f32[256]{0:T(256)S(1)}, f32[256]{0:T(256)}, u32[]{:S(2)}) copy-start(f32[256]{0:T(256)} %param.25) | copy-start | bytes 3076
Sparse Core Ops, SparseCore 0:
  10.4 57.0 all-gather.2
  69.2 53.8 all-gather.4
  138.3 154.0 reduce-scatter.2
  341.8 54.8 reduce-scatter.4
where the time goes:
time: 406 us; the launch traced here: 405 us
  waiting for transfers between devices  227 us (56%)
  other arithmetic  125 us (31%)
  matrix products  27.2 us (7%)
  between operations  14 us (3%)
  local copies, waits for them, and re-layouts  8.16 us (2%)
    reduce_scatter x1, waiting for transfers between devices, per_device(): lax.psum_scatter(jnp.einsum('hqd,hdc->cq', heads_out, columns, preferred_...  72.1 us
    add x16, other arithmetic, add_pole(): total + residue[None, None, :] * jnp.exp(-rate[None, None, :] * safe_diff...  64.9 us
    reduce_scatter x1, waiting for transfers between devices, per_device(): lax.psum_scatter(jnp.einsum('inc,jnc->jic', long_powers, states, precisio...  55 us
    all_gather x1, waiting for transfers between devices, attend(): lax.all_gather(key_rows, 'ctx', axis=0, tiled=True)  54.2 us
    all_gather x1, waiting for transfers between devices, attend(): lax.all_gather(value_rows, 'ctx', axis=0, tiled=True)  44.5 us
    dot_general x8, other arithmetic, modal_step(): local = jnp.einsum('ijc,jc->ic', toeplitz, piece, precision=highest)  22.6 us
    dot_general x1, matrix products, per_device(): jnp.einsum('hqd,hdc->cq', heads_out, columns, preferred_element_type=jnp....  15 us
    neg x16, other arithmetic, add_pole(): -rate[None, None, :] * safe_diff[:, :, None]  11.3 us
  transfers between devices with their start and end apart: 5, of which 5 were waited for; matrix products, arithmetic and copies ran while one was open for 24% of the time, Pallas kernels for 0%

commit v1 on v0

--- a/solution.py
+++ b/solution.py
@@ -6,6 +6,11 @@
 HD = 128
 BLOCK = 64
 masked_floor = -1e30
+
+
+def swapped_in(value, name, dim):
+    sent = jnp.stack([value] * lax.axis_size(name))
+    return jnp.concatenate(lax.all_to_all(sent, name, 0, 0), axis=dim)
 
 
 def from_behind(value, axis, steps):
@@ -90,10 +95,7 @@
             for rows_q, pos_q in groups
         )
     )
-    pieces = (
-        lax.all_gather(key_rows, "ctx", axis=0, tiled=True),
-        lax.all_gather(value_rows, "ctx", axis=0, tiled=True),
-    )
+    pieces = (lax.all_gather(key_rows, "ctx", axis=0, tiled=True), swapped_in(value_rows, "ctx", 0))
     count = pieces[0].shape[0]
     blocks = count // count
     keys_all = pieces[0].reshape(blocks, count, heads, HD)

time: 406 us -> 377 us (0.929)
  waiting for transfers between devices: 227 us -> 201 us
  other arithmetic: 125 us -> 113 us
  starting transfers between devices: 3.65 us -> 9.3 us
  local copies, waits for them, and re-layouts: 8.16 us -> 12.4 us
    all_gather x1 -> x0, waiting for transfers between devices: 44.5 us -> none  [attend(): lax.all_gather(value_rows, 'ctx', axis=0, tiled=True)]
    all_to_all x0 -> x1, waiting for transfers between devices: none -> 33.2 us  [swapped_in(): return jnp.concatenate(lax.all_to_all(sent, name, 0, 0), axis=dim)]
    all_gather x1, waiting for transfers between devices: 54.2 us -> 26 us  [attend(): lax.all_gather(key_rows, 'ctx', axis=0, tiled=True)]
    reduce_scatter x1, waiting for transfers between devices: 72.1 us -> 85.3 us  [per_device(): lax.psum_scatter(jnp.einsum('hqd,hdc->cq', heads_out, columns, preferred_...]
    neg x16, other arithmetic: 11.3 us -> 0.11 us  [add_pole(): -rate[None, None, :] * safe_diff[:, :, None]]
    all_to_all x0 -> x1, starting transfers between devices: none -> 5.73 us  [swapped_in(): return jnp.concatenate(lax.all_to_all(sent, name, 0, 0), axis=dim)]
  transfers between devices with their start and end apart: 5 -> 5, of which waited for: 5 -> 5; matrix products, arithmetic and copies ran while one was open for 24% -> 21% of each run, Pallas kernels for 0% -> 0%
where the time goes in v1:
time: 377 us; the launch traced here: 376 us
  waiting for transfers between devices  201 us (53%)
  other arithmetic  113 us (30%)
  matrix products  26.6 us (7%)
  between operations  14 us (4%)
  local copies, waits for them, and re-layouts  12.4 us (3%)
  starting transfers between devices  9.3 us (2%)
    reduce_scatter x1, waiting for transfers between devices, per_device(): lax.psum_scatter(jnp.einsum('hqd,hdc->cq', heads_out, columns, preferred_...  85.3 us
    add x16, other arithmetic, add_pole(): total + residue[None, None, :] * jnp.exp(-rate[None, None, :] * safe_diff...  64.9 us
    reduce_scatter x1, waiting for transfers between devices, per_device(): lax.psum_scatter(jnp.einsum('inc,jnc->jic', long_powers, states, precisio...  54.6 us
    all_to_all x1, waiting for transfers between devices, swapped_in(): return jnp.concatenate(lax.all_to_all(sent, name, 0, 0), axis=dim)  33.2 us
    all_gather x1, waiting for transfers between devices, attend(): lax.all_gather(key_rows, 'ctx', axis=0, tiled=True)  26 us
    dot_general x8, other arithmetic, modal_step(): local = jnp.einsum('ijc,jc->ic', toeplitz, piece, precision=highest)  22.7 us
    dot_general x1, matrix products, per_device(): jnp.einsum('hqd,hdc->cq', heads_out, columns, preferred_element_type=jnp....  15.3 us
  transfers between devices with their start and end apart: 5, of which 5 were waited for; matrix products, arithmetic and copies ran while one was open for 21% of the time, Pallas kernels for 0%

profile of v1, /device:TPU:26, one launch (start us, length us, event | category | flops | bytes accessed | tf_op | source)
XLA Modules:
  0.0 376.5 jit_solution(12110629122724123308)
XLA Ops:
  7.2 1.8 copy.19
  9.1 2.4 stack.2
  11.5 5.7 %all-to-all-start = ((bf16[8,512,256]{2,1,0:T(8,128)(2,1)}), bf16[8,512,256]{2,1,0:T(8,128)(2,1)}, u32[]{:S(2)}, u32[]{:S(2)}) async-start(bf16[8,512,256]{2,1,0:T(8,128)(2,1)} %stack.2), calls=%async_computation | async-start | bytes 4194304 | tf_op jit(solution)/shard_map/all_to_all | solution.py:13
  17.4 1.7 iota_compare_fusion
  19.1 33.2 %all-to-all-done = bf16[8,512,256]{2,1,0:T(8,128)(2,1)} async-done(((bf16[8,512,256]{2,1,0:T(8,128)(2,1)}), bf16[8,512,256]{2,1,0:T(8,128)(2,1)}, u32[]{:S(2)}, u32[]{:S(2)}) %all-to-all-start) | async-done | bytes 2097184 | tf_op jit(solution)/shard_map/all_to_all | solution.py:13
  52.3 4.0 %squeeze.19 = bf16[4096,2,128]{2,1,0:T(2,128)(2,1)} reshape(bf16[8,512,256]{2,1,0:T(8,128)(2,1)} %all-to-all-done) | data formatting | bytes 4194304 | tf_op jit(solution)/shard_map/while/body/jit(dynamic_index_in_dim)/squeeze | solution.py:125
  56.3 26.0 %all-gather.2.cloned.1.call-done = bf16[4096,256]{0,1:T(8,128)(2,1)} async-done(((bf16[512,256]{0,1:T(8,128)(2,1)}), bf16[4096,256]{0,1:T(8,128)(2,1)}) %all-gather.2.cloned.1.call-update) | async-done | bytes 2097168 | tf_op jit(solution)/shard_map/all_gather | solution.py:98
  82.2 5.4 %fusion.6 = (f32[2,512]{1,0:T(2,128)S(1)}, f32[2,512,4096]{2,1,0:T(8,128)S(1)}) fusion(pred[512,4096]{1,0:T(8,128)(4,1)S(1)} %iota_compare_fusion, bf16[4096,2,128]{0,2,1:T(8,128)(2,1)} %bitcast.86, bf16[512,256]{1,0:T(8,128)(2,1)S(1)} %copy-done), kind=kOutput, calls=%fused_computation.17 | convolution fusion | flops 1086323712 | bytes 21237760 | tf_op jit(solution)/shard_map/while/body/eval_jaxpr/qhd,khd->hqk/dot_general | solution.py:71
  87.7 5.3 %fusion.7 = f32[2,512]{1,0:T(2,128)S(1)} fusion(f32[2,512,4096]{2,1,0:T(8,128)S(1)} %get-tuple-element.265, f32[2,512]{1,0:T(2,128)S(1)} %broadcast_maximum_fusion, pred[512,4096]{1,0:T(8,128)(4,1)S(1)} %iota_compare_fusion), kind=kLoop, calls=%fused_computation.18 | loop fusion | flops 20970496 | bytes 18882560 | tf_op jit(solution)/shard_map/while/body/eval_jaxpr/reduce_sum | solution.py:79
  93.0 0.4 copy-done.1
  93.4 15.3 %fusion.9 = bf16[8192,512]{0,1:T(8,128)(2,1)} fusion(bf16[2,128,8192]{2,1,0:T(8,128)(2,1)} %bitcast.85, bf16[4096,2,128]{2,1,0:T(2,128)(2,1)} %squeeze.19, f32[2,512,4096]{2,1,0:T(8,128)} %copy-done.1, f32[2,512]{1,0:T(2,128)S(1)} %broadcast_maximum_fusion, pred[512,4096]{1,0:T(8,128)(4,1)S(1)} %iota_compare_fusion, f32[2,512]{1,0:T(2,128)S(1)} %get-tuple-element.263, ...), kind=kOutput, calls=%fused_computation.20 | convolution fusion | flops 3246784512 | bytes 33566720 | tf_op jit(solution)/shard_map/hqd,hdc->cq/dot_general | solution.py:150
  108.8 0.6 copy-done.3
  109.4 66.4 %while.32 = (s32[]{:T(128)}, f32[64,64,256]{2,1,0:T(8,128)}, f32[16,256]{1,0:T(8,128)S(1)}, f32[16,256]{1,0:T(8,128)S(1)}, f32[64]{0:T(128)S(1)}, /*index=5*/s32[]{:T(128)}, s32[]{:T(128)}) while((s32[]{:T(128)}, f32[64,64,256]{2,1,0:T(8,128)}, f32[16,256]{1,0:T(8,128)S(1)}, f32[16,256]{1,0:T(8,128)S(1)}, f32[64]{0:T(128)S(1)}, ...), condition=%wide.region_4.5_spmd.clone, body=%wide.region_3.4_spmd.clone.sunk | while | flops 4202755 | bytes 8427867 | solution.py:36
  109.5 2.5 select_add_fusion.2
  112.1 4.1 %select_add_fusion.2 = f32[64,64,256]{2,1,0:T(8,128)} fusion(f32[64,64,256]{2,1,0:T(8,128)} %get-tuple-element.374, f32[64,64]{1,0:T(8,128)S(1)} %subtract_maximum_fusion.2, f32[256]{0:T(256)S(1)} %bitcast.80, f32[256]{0:T(256)S(1)} %bitcast.81, pred[]{:T(512)S(6)} %compare.8), kind=kLoop, calls=%fused_computation.3.clone.1 | loop fusion | flops 4194304 | bytes 8407041 | tf_op jit(solution)/shard_map/while/body/eval_jaxpr/add | solution.py:32
  116.2 4.1 %select_add_fusion.2 = f32[64,64,256]{2,1,0:T(8,128)} fusion(f32[64,64,256]{2,1,0:T(8,128)} %get-tuple-element.374, f32[64,64]{1,0:T(8,128)S(1)} %subtract_maximum_fusion.2, f32[256]{0:T(256)S(1)} %bitcast.80, f32[256]{0:T(256)S(1)} %bitcast.81, pred[]{:T(512)S(6)} %compare.8), kind=kLoop, calls=%fused_computation.3.clone.1 | loop fusion | flops 4194304 | bytes 8407041 | tf_op jit(solution)/shard_map/while/body/eval_jaxpr/add | solution.py:32
  120.4 4.1 %select_add_fusion.2 = f32[64,64,256]{2,1,0:T(8,128)} fusion(f32[64,64,256]{2,1,0:T(8,128)} %get-tuple-element.374, f32[64,64]{1,0:T(8,128)S(1)} %subtract_maximum_fusion.2, f32[256]{0:T(256)S(1)} %bitcast.80, f32[256]{0:T(256)S(1)} %bitcast.81, pred[]{:T(512)S(6)} %compare.8), kind=kLoop, calls=%fused_computation.3.clone.1 | loop fusion | flops 4194304 | bytes 8407041 | tf_op jit(solution)/shard_map/while/body/eval_jaxpr/add | solution.py:32
  124.6 4.3 %select_add_fusion.2 = f32[64,64,256]{2,1,0:T(8,128)} fusion(f32[64,64,256]{2,1,0:T(8,128)} %get-tuple-element.374, f32[64,64]{1,0:T(8,128)S(1)} %subtract_maximum_fusion.2, f32[256]{0:T(256)S(1)} %bitcast.80, f32[256]{0:T(256)S(1)} %bitcast.81, pred[]{:T(512)S(6)} %compare.8), kind=kLoop, calls=%fused_computation.3.clone.1 | loop fusion | flops 4194304 | bytes 8407041 | tf_op jit(solution)/shard_map/while/body/eval_jaxpr/add | solution.py:32
  128.9 4.3 %select_add_fusion.2 = f32[64,64,256]{2,1,0:T(8,128)} fusion(f32[64,64,256]{2,1,0:T(8,128)} %get-tuple-element.374, f32[64,64]{1,0:T(8,128)S(1)} %subtract_maximum_fusion.2, f32[256]{0:T(256)S(1)} %bitcast.80, f32[256]{0:T(256)S(1)} %bitcast.81, pred[]{:T(512)S(6)} %compare.8), kind=kLoop, calls=%fused_computation.3.clone.1 | loop fusion | flops 4194304 | bytes 8407041 | tf_op jit(solution)/shard_map/while/body/eval_jaxpr/add | solution.py:32
  133.3 4.3 %select_add_fusion.2 = f32[64,64,256]{2,1,0:T(8,128)} fusion(f32[64,64,256]{2,1,0:T(8,128)} %get-tuple-element.374, f32[64,64]{1,0:T(8,128)S(1)} %subtract_maximum_fusion.2, f32[256]{0:T(256)S(1)} %bitcast.80, f32[256]{0:T(256)S(1)} %bitcast.81, pred[]{:T(512)S(6)} %compare.8), kind=kLoop, calls=%fused_computation.3.clone.1 | loop fusion | flops 4194304 | bytes 8407041 | tf_op jit(solution)/shard_map/while/body/eval_jaxpr/add | solution.py:32
  137.7 4.3 %select_add_fusion.2 = f32[64,64,256]{2,1,0:T(8,128)} fusion(f32[64,64,256]{2,1,0:T(8,128)} %get-tuple-element.374, f32[64,64]{1,0:T(8,128)S(1)} %subtract_maximum_fusion.2, f32[256]{0:T(256)S(1)} %bitcast.80, f32[256]{0:T(256)S(1)} %bitcast.81, pred[]{:T(512)S(6)} %compare.8), kind=kLoop, calls=%fused_computation.3.clone.1 | loop fusion | flops 4194304 | bytes 8407041 | tf_op jit(solution)/shard_map/while/body/eval_jaxpr/add | solution.py:32
  142.0 4.3 %select_add_fusion.2 = f32[64,64,256]{2,1,0:T(8,128)} fusion(f32[64,64,256]{2,1,0:T(8,128)} %get-tuple-element.374, f32[64,64]{1,0:T(8,128)S(1)} %subtract_maximum_fusion.2, f32[256]{0:T(256)S(1)} %bitcast.80, f32[256]{0:T(256)S(1)} %bitcast.81, pred[]{:T(512)S(6)} %compare.8), kind=kLoop, calls=%fused_computation.3.clone.1 | loop fusion | flops 4194304 | bytes 8407041 | tf_op jit(solution)/shard_map/while/body/eval_jaxpr/add | solution.py:32
  146.4 4.3 %select_add_fusion.2 = f32[64,64,256]{2,1,0:T(8,128)} fusion(f32[64,64,256]{2,1,0:T(8,128)} %get-tuple-element.374, f32[64,64]{1,0:T(8,128)S(1)} %subtract_maximum_fusion.2, f32[256]{0:T(256)S(1)} %bitcast.80, f32[256]{0:T(256)S(1)} %bitcast.81, pred[]{:T(512)S(6)} %compare.8), kind=kLoop, calls=%fused_computation.3.clone.1 | loop fusion | flops 4194304 | bytes 8407041 | tf_op jit(solution)/shard_map/while/body/eval_jaxpr/add | solution.py:32
  150.7 4.2 %select_add_fusion.2 = f32[64,64,256]{2,1,0:T(8,128)} fusion(f32[64,64,256]{2,1,0:T(8,128)} %get-tuple-element.374, f32[64,64]{1,0:T(8,128)S(1)} %subtract_maximum_fusion.2, f32[256]{0:T(256)S(1)} %bitcast.80, f32[256]{0:T(256)S(1)} %bitcast.81, pred[]{:T(512)S(6)} %compare.8), kind=kLoop, calls=%fused_computation.3.clone.1 | loop fusion | flops 4194304 | bytes 8407041 | tf_op jit(solution)/shard_map/while/body/eval_jaxpr/add | solution.py:32
  155.1 4.1 %select_add_fusion.2 = f32[64,64,256]{2,1,0:T(8,128)} fusion(f32[64,64,256]{2,1,0:T(8,128)} %get-tuple-element.374, f32[64,64]{1,0:T(8,128)S(1)} %subtract_maximum_fusion.2, f32[256]{0:T(256)S(1)} %bitcast.80, f32[256]{0:T(256)S(1)} %bitcast.81, pred[]{:T(512)S(6)} %compare.8), kind=kLoop, calls=%fused_computation.3.clone.1 | loop fusion | flops 4194304 | bytes 8407041 | tf_op jit(solution)/shard_map/while/body/eval_jaxpr/add | solution.py:32
  159.2 4.1 %select_add_fusion.2 = f32[64,64,256]{2,1,0:T(8,128)} fusion(f32[64,64,256]{2,1,0:T(8,128)} %get-tuple-element.374, f32[64,64]{1,0:T(8,128)S(1)} %subtract_maximum_fusion.2, f32[256]{0:T(256)S(1)} %bitcast.80, f32[256]{0:T(256)S(1)} %bitcast.81, pred[]{:T(512)S(6)} %compare.8), kind=kLoop, calls=%fused_computation.3.clone.1 | loop fusion | flops 4194304 | bytes 8407041 | tf_op jit(solution)/shard_map/while/body/eval_jaxpr/add | solution.py:32
  163.4 4.1 %select_add_fusion.2 = f32[64,64,256]{2,1,0:T(8,128)} fusion(f32[64,64,256]{2,1,0:T(8,128)} %get-tuple-element.374, f32[64,64]{1,0:T(8,128)S(1)} %subtract_maximum_fusion.2, f32[256]{0:T(256)S(1)} %bitcast.80, f32[256]{0:T(256)S(1)} %bitcast.81, pred[]{:T(512)S(6)} %compare.8), kind=kLoop, calls=%fused_computation.3.clone.1 | loop fusion | flops 4194304 | bytes 8407041 | tf_op jit(solution)/shard_map/while/body/eval_jaxpr/add | solution.py:32
  167.6 4.1 %select_add_fusion.2 = f32[64,64,256]{2,1,0:T(8,128)} fusion(f32[64,64,256]{2,1,0:T(8,128)} %get-tuple-element.374, f32[64,64]{1,0:T(8,128)S(1)} %subtract_maximum_fusion.2, f32[256]{0:T(256)S(1)} %bitcast.80, f32[256]{0:T(256)S(1)} %bitcast.81, pred[]{:T(512)S(6)} %compare.8), kind=kLoop, calls=%fused_computation.3.clone.1 | loop fusion | flops 4194304 | bytes 8407041 | tf_op jit(solution)/shard_map/while/body/eval_jaxpr/add | solution.py:32
  171.7 4.1 %select_add_fusion.2 = f32[64,64,256]{2,1,0:T(8,128)} fusion(f32[64,64,256]{2,1,0:T(8,128)} %get-tuple-element.374, f32[64,64]{1,0:T(8,128)S(1)} %subtract_maximum_fusion.2, f32[256]{0:T(256)S(1)} %bitcast.80, f32[256]{0:T(256)S(1)} %bitcast.81, pred[]{:T(512)S(6)} %compare.8), kind=kLoop, calls=%fused_computation.3.clone.1 | loop fusion | flops 4194304 | bytes 8407041 | tf_op jit(solution)/shard_map/while/body/eval_jaxpr/add | solution.py:32
  175.8 4.0 %broadcast_select_fusion = f32[64,64,256]{2,1,0:T(8,128)} fusion(f32[64,64,256]{2,1,0:T(8,128)} %get-tuple-element.104, pred[64,64]{1,0:T(8,128)(4,1)S(1)} %subtract_compare_fusion), kind=kLoop, calls=%fused_computation.33 | loop fusion | flops 1048576 | bytes 8392704 | tf_op jit(solution)/shard_map/jit(_where)/select_n | solution.py:39
  179.8 85.3 %reduce-scatter.3.cloned.1.call-done = bf16[256,512]{0,1:T(8,128)(2,1)} async-done(((bf16[8192,512]{0,1:T(8,128)(2,1)}), bf16[256,512]{0,1:T(8,128)(2,1)}) %reduce-scatter.3.cloned.1.call-update) | async-done | bytes 262160 | tf_op jit(solution)/shard_map/reduce_scatter | solution.py:149
  265.0 1.0 fusion.48
  266.1 3.5 collective-permute-start
  269.8 1.7 collective-permute-done
  271.8 32.8 %while.33 = (s32[]{:T(128)}, f32[16,256]{1,0:T(8,128)S(1)}, f32[8,64,256]{2,1,0:T(8,128)}, f32[16,256]{1,0:T(8,128)S(1)}, f32[8,64,256]{2,1,0:T(8,128)S(1)}, /*i...) while((s32[]{:T(128)}, f32[16,256]{1,0:T(8,128)S(1)}, ...), condition=%wide.region_6.7_spmd.clone.clone.clone, body=%wide.region_5.6_spmd.clone.clone.clone.sunk | while | flops 3665923 | bytes 4949123 | solution.py:58
  271.8 0.2 multiply_reduce_fusion.6
  272.1 0.3 multiply_reduce_fusion.8
  272.5 2.8 multiply_reduce_fusion.7
  275.3 0.6 bitcast_dynamic-update-slice_fusion.2
  276.2 0.3 multiply_reduce_fusion.8
  276.6 2.8 multiply_reduce_fusion.7
  279.4 0.6 bitcast_dynamic-update-slice_fusion.2
  280.3 0.3 multiply_reduce_fusion.8
  280.7 2.8 multiply_reduce_fusion.7
  283.5 0.6 bitcast_dynamic-update-slice_fusion.2
  284.4 0.3 multiply_reduce_fusion.8
  284.8 2.8 multiply_reduce_fusion.7
  287.6 0.6 bitcast_dynamic-update-slice_fusion.2
  288.5 0.3 multiply_reduce_fusion.8
  288.9 2.8 multiply_reduce_fusion.7
  291.7 0.6 bitcast_dynamic-update-slice_fusion.2
  292.6 0.3 multiply_reduce_fusion.8
  293.0 2.8 multiply_reduce_fusion.7
  295.8 0.6 bitcast_dynamic-update-slice_fusion.2
  296.7 0.3 multiply_reduce_fusion.8
  297.1 2.8 multiply_reduce_fusion.7
  299.9 0.6 bitcast_dynamic-update-slice_fusion.2
  300.8 0.3 multiply_reduce_fusion.8
  301.2 2.8 multiply_reduce_fusion.7
  304.0 0.6 bitcast_dynamic-update-slice_fusion.2
  304.7 5.9 %convert_bitcast_fusion = bf16[8,512,256]{1,0,2:T(8,128)(2,1)S(1)} fusion(f32[512]{0:T(512)S(1)} %iota_convert_fusion, f32[16,256]{0,1:T(8,128)S(1)} %copy.22, f32[16,256]{0,1:T(8,128)S(1)} %copy.24, f32[16,256]{0,1:T(8,128)S(1)} %copy.23, f32[8]{0:T(128)S(1)} %maximum_convert_fusion.1, pred[8]{0:T(512)(128)(4,1)S(1)} %iota_compare_fusion.1), kind=kOutput, calls=%fused_computation.32 | convolution fusion | flops 206667776 | bytes 2148392 | tf_op jit(solution)/shard_map/inc,jnc->jic/dot_general | solution.py:177
  310.6 2.8 copy.26
  313.4 54.6 %reduce-scatter.5.cloned.1.call-done = bf16[512,256]{1,0:T(8,128)(2,1)} async-done(((bf16[4096,256]{1,0:T(8,128)(2,1)}), bf16[512,256]{1,0:T(8,128)(2,1)}) %reduce-scatter.5.cloned.1.call-update) | async-done | bytes 262160 | tf_op jit(solution)/shard_map/reduce_scatter | solution.py:176
  368.0 1.9 fusion.47
  (99 shorter events, 4.0 us)
Async XLA Ops:
  7.2 75.1 %copy-start = (bf16[512,256]{1,0:T(8,128)(2,1)S(1)}, bf16[512,256]{1,0:T(8,128)(2,1)}, u32[]{:S(2)}) copy-start(bf16[512,256]{1,0:T(8,128)(2,1)} %param.16) | copy-start | bytes 786436
  7.2 10.1 %copy-start.8 = (f32[3,256]{1,0:T(4,128)S(1)}, f32[3,256]{1,0:T(4,128)}, u32[]{:S(2)}) copy-start(f32[3,256]{1,0:T(4,128)} %param.22) | copy-start | bytes 9220
  7.2 10.2 %copy-start.7 = (f32[16,256]{1,0:T(8,128)S(1)}, f32[16,256]{1,0:T(8,128)}, u32[]{:S(2)}) copy-start(f32[16,256]{1,0:T(8,128)} %param.23) | copy-start | bytes 49156
  7.2 75.0 %all-gather.2.cloned.1.call-start = ((), (), s32[]{:S(2)}) async-start(), calls=%async_computation.3 | async-start | bytes 2359296 | tf_op jit(solution)/shard_map/all_gather | solution.py:98
  11.5 40.8 %all-to-all-start = ((bf16[8,512,256]{2,1,0:T(8,128)(2,1)}), bf16[8,512,256]{2,1,0:T(8,128)(2,1)}, u32[]{:S(2)}, u32[]{:S(2)}) async-start(bf16[8,512,256]{2,1,0:T(8,128)(2,1)} %stack.2), calls=%async_computation | async-start | bytes 4194304 | tf_op jit(solution)/shard_map/all_to_all | solution.py:13
  17.2 247.8 %reduce-scatter.3.cloned.1.call-start = ((), (), s32[]{:S(2)}) async-start(), calls=%async_computation.4 | async-start | bytes 8650752 | tf_op jit(solution)/shard_map/reduce_scatter | solution.py:149
  87.7 5.7 %copy-start.1 = (f32[2,512,4096]{2,1,0:T(8,128)}, f32[2,512,4096]{2,1,0:T(8,128)S(1)}, u32[]{:S(2)}) copy-start(f32[2,512,4096]{2,1,0:T(8,128)S(1)} %get-tuple-element.265) | copy-start | bytes 50331652
  108.7 0.7 copy-start.3
  108.7 259.3 %reduce-scatter.5.cloned.1.call-start = ((), (), s32[]{:S(2)}) async-start(), calls=%async_computation.5 | async-start | bytes 2359296 | tf_op jit(solution)/shard_map/reduce_scatter | solution.py:176
  175.8 89.2 %copy-start.5 = (bf16[512,256]{1,0:T(8,128)(2,1)S(1)}, bf16[512,256]{1,0:T(8,128)(2,1)}, u32[]{:S(2)}) copy-start(bf16[512,256]{1,0:T(8,128)(2,1)} %param.15) | copy-start | bytes 786436
  175.8 95.8 %copy-start.6 = (bf16[512,256]{1,0:T(8,128)(2,1)S(1)}, bf16[512,256]{1,0:T(8,128)(2,1)}, u32[]{:S(2)}) copy-start(bf16[512,256]{1,0:T(8,128)(2,1)} %param.20) | copy-start | bytes 786436
  266.0 5.8 %copy-start.2 = (bf16[512,256]{1,0:T(8,128)(2,1)}, bf16[512,256]{1,0:T(8,128)(2,1)S(1)}, u32[]{:S(2)}) copy-start(bf16[512,256]{1,0:T(8,128)(2,1)S(1)} %fusion.48) | copy-start | bytes 786436
  266.1 5.5 %collective-permute-start = (bf16[2,256]{1,0:T(2,128)(2,1)S(1)}, bf16[2,256]{1,0:T(2,128)(2,1)S(1)}, u32[]{:S(2)}, u32[]{:S(2)}) collective-permute-start(bf16[2,256]{1,0:T(2,128)(2,1)S(1)} %slice.28), channel_id=1, source_target_pairs={{0,32},{32,64},{64,96},{96,128},{128,160},{160,192},{192,224},{1,3... | collective-permute-start | bytes 3080 | tf_op jit(solution)/shard_map/ppermute | solution.py:19
  310.6 57.4 %copy-start.4 = (f32[8,64,256]{2,1,0:T(8,128)S(1)}, f32[8,64,256]{2,1,0:T(8,128)}, u32[]{:S(2)}) copy-start(f32[8,64,256]{2,1,0:T(8,128)} %get-tuple-element.105) | copy-start | bytes 1572868
  310.6 57.4 %copy-start.9 = (f32[256]{0:T(256)S(1)}, f32[256]{0:T(256)}, u32[]{:S(2)}) copy-start(f32[256]{0:T(256)} %param.25) | copy-start | bytes 3076
Sparse Core Ops, SparseCore 0:
  10.4 71.8 all-gather.1
  108.8 156.1 reduce-scatter.2
  313.6 54.4 reduce-scatter.4
